TPU v7x, 32 devices: a whole 2x2x4 slice. The times are simulated.
32 devices in a mesh: section: 4 (over y, x), tok: 4 (over z), head: 2 (over core).
Axes of the slice: x: 2, y: 2, z: 4, core: 2. Of those that a mesh axis runs over, the one named last changes fastest.
Arguments:
- group_in: bfloat16 [4, 512, 2048], P('section', 'tok'), may hold values from -6 to 6
- w_qkv: bfloat16 [4, 3, 2048, 2048], P('section', None, 'tok', 'head'), may hold values from -0.125 to 0.125
- w_out: bfloat16 [4, 2048, 2048], P('section', 'head', 'tok'), may hold values from -0.125 to 0.125
- step_sizes: float32 [4, 512, 4], P('section', 'tok', 'head'), may hold values from 0.05 to 1
- fast_weights: bfloat16 [4, 4, 3, 512, 512], P('section', 'head'), may hold values from -0.25 to 0.25
- momentum: bfloat16 [4, 4, 3, 512, 512], P('section', 'head'), may hold values from -16 to 16
- momentum_decay: float32 [4, 4], P('section', 'head'), may hold values from 0.5 to 0.95
- fast_rate: float32 [4, 4], P('section', 'head'), may hold values from 0.3 to 1
Outputs:
- handed: bfloat16 [4, 512, 2048], P('section', 'tok', 'head')
- fast_next: bfloat16 [4, 4, 3, 512, 512], P('section', 'head')
All inputs are finite; a program needn't handle non-finite values.
Results may differ from a plain program's by a relative error of at most 0.015.
Values may be sent and summed in bfloat16 or wider, within the bound.
A program may use at most 128 MiB of HBM per device.

v0:
```python
import jax
import jax.numpy as jnp
from jax import lax
from jax.sharding import PartitionSpec as P

NS_ITERS = 2
coef_linear = 3.4445
coef_cubic = -4.775
coef_quintic = 2.0315


def passed_along(value, axis, steps):
    count = lax.axis_size(axis)
    pairs = [(source, (source + steps) % count) for source in range(count)]
    return lax.ppermute(value, axis, pairs)


def rms_rows(values_in, epsilon):
    return values_in * lax.rsqrt(jnp.mean(values_in * values_in, axis=-1, keepdims=True) + epsilon)


def fast_grads(key_rows, value_rows, step_rates, weights):
    gate_pre = jnp.einsum(
        "thi,hij->thj", key_rows, weights[:, 0], preferred_element_type=jnp.float32
    )
    up_pre = jnp.einsum("thi,hij->thj", key_rows, weights[:, 1], preferred_element_type=jnp.float32)
    squash = jax.nn.sigmoid(gate_pre)
    hidden = (gate_pre * squash * up_pre).astype(jnp.bfloat16)
    errors = (-(step_rates[:, :, None] * value_rows.astype(jnp.float32))).astype(jnp.bfloat16)
    back_hidden = jnp.einsum(
        "thi,hij->thj", errors, weights[:, 2], preferred_element_type=jnp.float32
    )
    grad_gate = (back_hidden * up_pre * squash * (1.0 + gate_pre * (1.0 - squash))).astype(
        jnp.bfloat16
    )
    grad_up = (back_hidden * gate_pre * squash).astype(jnp.bfloat16)
    grad_first = jnp.einsum("thi,thj->hij", key_rows, grad_gate, preferred_element_type=jnp.float32)
    grad_third = jnp.einsum("thi,thj->hij", key_rows, grad_up, preferred_element_type=jnp.float32)
    grad_second = jnp.einsum("thi,thj->hij", errors, hidden, preferred_element_type=jnp.float32)
    return jnp.stack([grad_first, grad_third, grad_second], axis=1)


def newton_step(rows_in, gathered):
    gram_matrix = jnp.einsum(
        "mij,mik->mjk", gathered, gathered, preferred_element_type=jnp.float32
    ).astype(jnp.bfloat16)
    cubic_term = jnp.einsum(
        "mij,mjk->mik", rows_in, gram_matrix, preferred_element_type=jnp.float32
    )
    quintic_term = jnp.einsum(
        "mij,mjk->mik",
        cubic_term.astype(jnp.bfloat16),
        gram_matrix,
        preferred_element_type=jnp.float32,
    )
    return (
        coef_linear * rows_in.astype(jnp.float32)
        + coef_cubic * cubic_term
        + coef_quintic * quintic_term
    ).astype(jnp.bfloat16)


def apply_fast(queries, updated):
    gate_pre = jnp.einsum(
        "thi,hij->thj", queries, updated[:, 0], preferred_element_type=jnp.float32
    )
    up_pre = jnp.einsum("thi,hij->thj", queries, updated[:, 1], preferred_element_type=jnp.float32)
    hidden = (jax.nn.silu(gate_pre) * up_pre).astype(jnp.bfloat16)
    output = jnp.einsum("thj,hij->thi", hidden, updated[:, 2], preferred_element_type=jnp.float32)
    return rms_rows(output, 1e-05).astype(jnp.bfloat16)


def shards(group_in, w_qkv, w_out, step_sizes, fast_weights, momentum, momentum_decay, fast_rate):
    tokens = group_in[0]
    tok_rows = tokens.shape[0]
    local_heads = fast_weights.shape[1]
    fan_width = fast_weights.shape[3]
    hid_width = fast_weights.shape[4]
    half_width = w_qkv.shape[3]
    columns = lax.all_to_all(tokens, "tok", split_axis=1, concat_axis=0, tiled=True)
    all_rows = columns.shape[0]
    rates = lax.all_gather(step_sizes[0], "tok", axis=0, tiled=True)
    partial_kv = jnp.einsum(
        "td,jde->jte", columns, w_qkv[0, 1:], preferred_element_type=jnp.float32
    ).astype(jnp.bfloat16)
    partial_q = jnp.dot(columns, w_qkv[0, 0], preferred_element_type=jnp.float32).astype(
        jnp.bfloat16
    )
    summed_kv = lax.psum(partial_kv, "tok").astype(jnp.float32)
    summed_q = lax.psum(partial_q, "tok").astype(jnp.float32)
    shaped = summed_kv.reshape(2, all_rows, local_heads, fan_width)
    key_rows = rms_rows(shaped[0], 1e-06).astype(jnp.bfloat16)
    value_rows = shaped[1].astype(jnp.bfloat16)
    queries = rms_rows(summed_q.reshape(all_rows, local_heads, fan_width), 1e-06).astype(
        jnp.bfloat16
    )
    summed = fast_grads(key_rows, value_rows, rates, fast_weights[0])
    decay_rate = momentum_decay[0][:, None, None, None]
    moment = decay_rate * momentum[0].astype(jnp.float32) + summed
    norm_values = jnp.sqrt(jnp.sum(moment * moment, axis=(2, 3), keepdims=True))
    iterate = (moment / (norm_values + 1e-06)).astype(jnp.bfloat16)
    iterate = iterate.reshape(local_heads * 3, fan_width, hid_width)
    for number in range(NS_ITERS):
        iterate = newton_step(iterate, iterate)
    iterate = iterate.reshape(local_heads, 3, fan_width, hid_width)
    updated = (
        fast_weights[0].astype(jnp.float32)
        - fast_rate[0][:, None, None, None] * iterate.astype(jnp.float32)
    ).astype(jnp.bfloat16)
    mixed_heads = apply_fast(queries, updated).reshape(all_rows, half_width)
    partial_out = jnp.dot(mixed_heads, w_out[0], preferred_element_type=jnp.float32)
    own_rows = lax.all_to_all(
        partial_out.astype(jnp.bfloat16), "tok", split_axis=0, concat_axis=1, tiled=True
    )
    summed_out = lax.psum_scatter(own_rows, "head", scatter_dimension=1, tiled=True).astype(
        jnp.float32
    )
    share_width = summed_out.shape[1]
    own_tokens = lax.dynamic_slice_in_dim(
        tokens, lax.axis_index("head") * share_width, share_width, 1
    )
    layer_out = (own_tokens.astype(jnp.float32) + summed_out).astype(jnp.bfloat16)
    handed = passed_along(layer_out[None], "section", 1)
    return (handed, updated[None])


def solution(mesh):
    placed = (
        P("section", "tok", None),
        P("section", None, "tok", "head"),
        P("section", "head", "tok"),
        P("section", "tok", "head"),
        P("section", "head", None, None, None),
        P("section", "head", None, None, None),
        P("section", "head"),
        P("section", "head"),
    )
    return jax.shard_map(
        shards,
        mesh=mesh,
        in_specs=placed,
        out_specs=(P("section", "tok", "head"), P("section", "head", None, None, None)),
        check_vma=False,
    )
```

profile of v0, /device:TPU:0, one launch (start us, length us, event | category | flops | bytes accessed | tf_op | source)
XLA Modules:
  0.0 256.0 jit_solution(371909318707594207)
XLA Ops:
  8.9 20.9 %all_to_all.38 = bf16[128,4,512]{2,0,1:T(8,128)(2,1)S(1)} all-to-all(bf16[128,4,512]{2,0,1:T(8,128)(2,1)S(1)} %copy.43), channel_id=1, replica_groups=mesh['section'=4,'tok'=4,'head'=2] {'tok'}, dimensions={1} | all-to-all | bytes 1048576 | tf_op jit(solution)/shard_map/all_to_all | solution.py:80
  29.8 1.9 convolution_convert_fusion.2
  32.8 2.7 %convert_bitcast_fusion = bf16[2,512,1024]{1,2,0:T(8,128)(2,1)} fusion(bf16[512,512,1]{1,0,2:T(8,128)(2,1)S(1)} %bitcast.205, bf16[1,3,512,1024]{3,2,1,0:T(8,128)(2,1)S(1)} %copy-done.10), kind=kOutput, calls=%fused_computation.64 | convolution fusion | flops 1074790400 | bytes 4718592 | tf_op jit(solution)/shard_map/td,jde->jte/dot_general | solution.py:83
  35.5 3.9 %copy.82 = bf16[1,2,3,512,512]{4,3,1,2,0:T(8,128)(2,1)} copy(bf16[1,2,3,512,512]{4,3,2,1,0:T(8,128)(2,1)} %param.12) | data formatting | bytes 6291456 | tf_op args[4]
  39.6 3.1 %copy_convert_fusion = f32[1,2,3,512,512]{4,3,1,2,0:T(8,128)S(1)} fusion(bf16[1,2,3,512,512]{4,3,2,1,0:T(8,128)(2,1)} %param.13), kind=kLoop, calls=%fused_computation.16 | loop fusion | flops 1572864 | bytes 9437184 | tf_op jit(solution)/shard_map/convert_element_type | solution.py:99
  42.8 3.4 %copy.41 = f32[1,2,3,512,512]{4,3,2,1,0:T(8,128)} copy(f32[1,2,3,512,512]{4,3,1,2,0:T(8,128)S(1)} %copy_convert_fusion) | data formatting | bytes 12582912 | tf_op jit(solution)/shard_map/convert_element_type | solution.py:99
  46.1 9.2 %all-gather = f32[1,512,2]{1,2,0:T(2,128)S(1)} all-gather(f32[1,128,2]{1,2,0:T(2,128)S(1)} %copy-done.8), channel_id=2, replica_groups=mesh['section'=4,'tok'=4,'head'=2] {'tok'}, dimensions={1}, use_global_device_ids=true | all-gather | bytes 5120 | tf_op jit(solution)/shard_map/all_gather | solution.py:82
  55.3 100.5 %all-reduce.3.cloned.1.call-done = (bf16[2,512,1024]{1,2,0:T(8,128)(2,1)}, bf16[512,2,512]{2,0,1:T(8,128)(2,1)}) async-done(((bf16[2,512,1024]{1,2,0:T(8,128)(2,1)}, bf16[512,2,512]{2,0,1:T(8,128)(2,1)}), (bf16[2,512,1024]{1,2,0:T(8,128)(2,1)}, bf16[512,2,512]{2,0,1:T(8,128)(2,1)})) %all-reduce.3.cloned.1.call-update) | async-done | bytes 3145744 | tf_op jit(solution)/shard_map/psum | solution.py:89
  155.8 1.8 fusion.71
  164.8 2.1 fusion.2
  166.9 3.4 %copy.47 = f32[2,3,512,512]{3,2,1,0:T(8,128)} copy(f32[2,3,512,512]{3,2,0,1:T(8,128)S(1)} %get-tuple-element.5) | data formatting | bytes 12582912 | tf_op jit(solution)/shard_map/stack | solution.py:40
  170.4 6.4 %fusion.4 = bf16[6,512,512]{2,1,0:T(8,128)(2,1)S(1)} fusion(f32[2,3,512,512]{3,2,1,0:T(8,128)} %copy.47, f32[1,2,3,512,512]{4,3,2,1,0:T(8,128)} %copy.41, f32[6]{0:T(128)S(1)} %add.85, f32[6]{0:T(128)S(1)} %mul.145), kind=kLoop, calls=%fused_computation.7 | loop fusion | flops 6291456 | bytes 15728688 | tf_op jit(solution)/shard_map/convert_element_type | solution.py:101
  176.8 1.8 convolution_convert_fusion.1
  178.6 4.5 %fusion.74 = f32[6,512,512]{2,1,0:T(8,128)} fusion(bf16[6,512,512]{2,1,0:T(8,128)(2,1)S(1)} %fusion.4, bf16[6,512,512]{2,1,0:T(8,128)(2,1)S(1)} %convolution_convert_fusion.1), kind=kOutput, calls=%fused_computation.99 | convolution fusion | flops 1610612736 | bytes 12582912 | tf_op jit(solution)/shard_map/mij,mjk->mik/dot_general | solution.py:47
  183.1 6.9 %add_convert_fusion.1 = bf16[6,512,512]{2,1,0:T(8,128)(2,1)S(1)} fusion(f32[6,512,512]{2,1,0:T(8,128)} %fusion.74, bf16[6,512,512]{2,1,0:T(8,128)(2,1)S(1)} %fusion.4, bf16[6,512,512]{2,1,0:T(8,128)(2,1)S(1)} %convolution_convert_fusion.1), kind=kOutput, calls=%fused_computation.14 | convolution fusion | flops 1623195648 | bytes 15728640 | tf_op jit(solution)/shard_map/mij,mjk->mik/dot_general | solution.py:50
  189.9 1.8 convolution_convert_fusion
  193.6 2.4 fusion.7
  196.4 5.0 %fusion.6 = bf16[2,3,512,512]{3,2,0,1:T(8,128)(2,1)S(1)} fusion(f32[2,3,512,512]{3,2,1,0:T(8,128)S(1)} %bitcast.187, f32[2]{0:T(128)S(1)} %bitcast.209, bf16[1,2,3,512,512]{4,3,2,1,0:T(8,128)(2,1)} %param.12), kind=kLoop, calls=%fused_computation.11 | loop fusion | flops 6291456 | bytes 12582920 | tf_op jit(solution)/shard_map/convert_element_type | solution.py:109
  203.1 2.1 fusion.45
  205.2 5.1 %fusion.24 = (f32[512,2]{0,1:T(2,128)S(1)}, f32[2,512,512]{2,1,0:T(8,128)}) fusion(f32[2,512,512]{1,2,0:T(8,128)} %fusion.45, bf16[2,3,512,512]{3,2,0,1:T(8,128)(2,1)} %copy-done.4, bf16[512,2,512]{2,0,1:T(8,128)(2,1)S(1)} %copy-done.5, f32[512,2]{0,1:T(2,128)S(1)} %add_rsqrt_fusion.1), kind=kOutput, calls=%fused_computation.39 | convolution fusion | flops 1079507968 | bytes 7348224 | tf_op jit(solution)/shard_map/thj,hij->thi/dot_general | solution.py:69
  210.3 1.9 fusion.25
  213.0 17.0 %all_to_all.39 = bf16[4,128,512]{2,1,0:T(8,128)(2,1)S(1)} all-to-all(bf16[4,128,512]{2,1,0:T(8,128)(2,1)S(1)} %bitcast.206), channel_id=1, replica_groups=mesh['section'=4,'tok'=4,'head'=2] {'tok'}, dimensions={0} | all-to-all | bytes 1048576 | tf_op jit(solution)/shard_map/all_to_all | solution.py:112
  230.9 7.2 %reduce-scatter.2.cloned.1.call-done = bf16[128,1024]{1,0:T(8,128)(2,1)} async-done(((bf16[128,2048]{1,0:T(8,128)(2,1)}), bf16[128,1024]{1,0:T(8,128)(2,1)}) %reduce-scatter.2.cloned.1.call-update) | async-done | bytes 262160 | tf_op jit(solution)/shard_map/reduce_scatter | solution.py:115
  240.8 6.5 %subtract_convert_fusion = bf16[1,2,3,512,512]{4,3,2,1,0:T(8,128)(2,1)} fusion(f32[1,2,3,512,512]{4,3,2,1,0:T(8,128)} %bitcast.188, bf16[1,2,3,512,512]{4,3,2,1,0:T(8,128)(2,1)} %param.12, f32[2]{0:T(128)S(1)} %bitcast.210), kind=kLoop, calls=%fused_computation.12 | loop fusion | flops 6291456 | bytes 12582920 | tf_op jit(solution)/shard_map/convert_element_type | solution.py:109
  (52 shorter events, 20.3 us)
Async XLA Ops:
  7.2 205.0 %copy-start = (bf16[1,1024,512]{2,1,0:T(8,128)(2,1)S(1)}, bf16[1,1024,512]{2,1,0:T(8,128)(2,1)}, u32[]{:S(2)}) copy-start(bf16[1,1024,512]{2,1,0:T(8,128)(2,1)} %param.10) | copy-start | bytes 3145732
  7.2 148.6 %all-reduce.3.cloned.1.call-start = ((), (), s32[]{:S(2)}) async-start(), calls=%async_computation.4 | async-start | bytes 6291456 | tf_op jit(solution)/shard_map/psum | solution.py:89
  8.8 23.9 %copy-start.10 = (bf16[1,3,512,1024]{3,2,1,0:T(8,128)(2,1)S(1)}, bf16[1,3,512,1024]{3,2,1,0:T(8,128)(2,1)}, u32[]{:S(2)}) copy-start(bf16[1,3,512,1024]{3,2,1,0:T(8,128)(2,1)} %param.9) | copy-start | bytes 9437188
  35.5 4.0 %copy-start.9 = (f32[1,2]{1,0:T(1,128)S(1)}, f32[1,2]{1,0:T(1,128)}, u32[]{:S(2)}) copy-start(f32[1,2]{1,0:T(1,128)} %param.14) | copy-start | bytes 28
  35.5 202.5 %reduce-scatter.2.cloned.1.call-start = ((), (), s32[]{:S(2)}) async-start(), calls=%async_computation.3 | async-start | bytes 786432 | tf_op jit(solution)/shard_map/reduce_scatter | solution.py:115
  42.8 3.4 %copy-start.8 = (f32[1,128,2]{1,2,0:T(2,128)S(1)}, f32[1,128,2]{1,2,0:T(2,128)}, u32[]{:S(2)}) copy-start(f32[1,128,2]{1,2,0:T(2,128)} %param.11) | copy-start | bytes 3076
  155.8 2.5 copy-start.3
  162.9 1.9 copy-start.2
  193.6 2.5 copy-start.5
  193.6 2.8 %copy-start.7 = (f32[1,2]{1,0:T(1,128)S(1)}, f32[1,2]{1,0:T(1,128)}, u32[]{:S(2)}) copy-start(f32[1,2]{1,0:T(1,128)} %param.15) | copy-start | bytes 28
  196.1 5.4 %copy-start.1 = (f32[6,512,512]{2,1,0:T(8,128)}, f32[6,512,512]{2,1,0:T(8,128)S(1)}, u32[]{:S(2)}) copy-start(f32[6,512,512]{2,1,0:T(8,128)S(1)} %fusion.7) | copy-start | bytes 18874372
  201.4 1.7 copy-start.4
  212.2 25.8 %copy-start.6 = (bf16[1,128,2048]{2,1,0:T(8,128)(2,1)S(1)}, bf16[1,128,2048]{2,1,0:T(8,128)(2,1)}, u32[]{:S(2)}) copy-start(bf16[1,128,2048]{2,1,0:T(8,128)(2,1)} %param.8) | copy-start | bytes 1572868
  239.0 9.5 %collective-permute-start = (bf16[1,128,1024]{2,1,0:T(8,128)(2,1)S(1)}, bf16[1,128,1024]{2,1,0:T(8,128)(2,1)S(1)}, u32[]{:S(2)}, u32[]{:S(2)}) collective-permute-start(bf16[1,128,1024]{2,1,0:T(8,128)(2,1)S(1)} %fusion.66), channel_id=1, source_target_pairs={{0,8},{8,16},{16,24},{24,0},{1,9},{9,17},{17,25},{25,1},{2,10},{10... | collective-permute-start | bytes 786440 | tf_op jit(solution)/shard_map/ppermute | solution.py:15
Sparse Core Ops, SparseCore 0:
  35.6 120.1 all-reduce.2
  231.0 6.9 reduce-scatter.1
where the time goes:
time: 257 us; the launch traced here: 256 us
  waiting for transfers between devices  109 us (42%)
  blocking collectives  47.1 us (18%)
  matrix products  37.3 us (15%)
  other arithmetic  26.5 us (10%)
  local copies, waits for them, and re-layouts  20.1 us (8%)
  between operations  14.3 us (6%)
    psum x1, waiting for transfers between devices, shards(): summed_kv = lax.psum(partial_kv, 'tok').astype(jnp.float32)  101 us
    all_to_all x1, blocking collectives, shards(): lax.all_to_all(tokens, 'tok', split_axis=1, concat_axis=0, tiled=True)  20.9 us
    all_to_all x1, blocking collectives, shards(): lax.all_to_all(partial_out.astype(jnp.bfloat16), 'tok', split_axis=0, con...  17 us
    convert_element_type x2, other arithmetic, shards(): updated = (fast_weights[0].astype(jnp.float32) - fast_rate[0][:, None, No...  11.5 us
    dot_general x2, matrix products, newton_step(): jnp.einsum('mij,mjk->mik', cubic_term.astype(jnp.bfloat16), gram_matrix,...  9.3 us
    all_gather x1, blocking collectives, shards(): rates = lax.all_gather(step_sizes[0], 'tok', axis=0, tiled=True)  9.16 us
    unnamed x24, local copies, waits for them, and re-layouts  7.67 us
    reduce_scatter x1, waiting for transfers between devices, shards(): lax.psum_scatter(own_rows, 'head', scatter_dimension=1, tiled=True)  7.15 us
  transfers between devices with their start and end apart: 3, of which 3 were waited for; matrix products, arithmetic and copies ran while one was open for 7% of the time, Pallas kernels for 0%

commit v1 on v0

--- a/solution.py
+++ b/solution.py
@@ -86,7 +86,7 @@
     partial_q = jnp.dot(columns, w_qkv[0, 0], preferred_element_type=jnp.float32).astype(
         jnp.bfloat16
     )
-    summed_kv = lax.psum(partial_kv, "tok").astype(jnp.float32)
+    summed_kv = jnp.sum(lax.all_gather(partial_kv, "tok"), axis=0).astype(jnp.float32)
     summed_q = lax.psum(partial_q, "tok").astype(jnp.float32)
     shaped = summed_kv.reshape(2, all_rows, local_heads, fan_width)
     key_rows = rms_rows(shaped[0], 1e-06).astype(jnp.bfloat16)

time: 257 us -> 356 us (1.39)
  waiting for transfers between devices: 109 us -> 183 us
  other arithmetic: 26.5 us -> 38.4 us
  local copies, waits for them, and re-layouts: 20.1 us -> 28.3 us
  matrix products: 37.3 us -> 42.4 us
    all_gather x0 -> x1, waiting for transfers between devices: none -> 149 us  [shards(): lax.all_gather(partial_kv, 'tok')]
    psum x1, waiting for transfers between devices: 101 us -> 25.8 us  [shards(): summed_q = lax.psum(partial_q, 'tok').astype(jnp.float32)]
    reduce_sum x0 -> x1, other arithmetic: none -> 6.31 us  [shards(): jnp.sum(lax.all_gather(partial_kv, 'tok'), axis=0).astype(jnp.float32)]
    convert_element_type x0 -> x2, local copies, waits for them, and re-layouts: none -> 5.36 us  [the longest x1 2.92 us: fast_grads(): value_rows.astype(jnp.float32)]
    convert_element_type x0 -> x2, other arithmetic: none -> 4.35 us  [the longest x1 2.41 us: fast_grads(): value_rows.astype(jnp.float32)]
    squeeze x0 -> x2, local copies, waits for them, and re-layouts: none -> 3.75 us  [shards(): key_rows = rms_rows(shaped[0], 1e-06).astype(jnp.bfloat16)]
    unnamed x24 -> x30, local copies, waits for them, and re-layouts: 7.67 us -> 8.54 us
  transfers between devices with their start and end apart: 3 -> 4, of which waited for: 3 -> 4; matrix products, arithmetic and copies ran while one was open for 7% -> 7% of each run, Pallas kernels for 0% -> 0%
where the time goes in v1:
time: 356 us
  waiting for transfers between devices  183 us (51%)
  blocking collectives  47.5 us (13%)
  matrix products  42.4 us (12%)
  other arithmetic  38.4 us (11%)
  local copies, waits for them, and re-layouts  28.3 us (8%)
  between operations  14 us (4%)
    all_gather x1, waiting for transfers between devices, shards(): lax.all_gather(partial_kv, 'tok')  149 us
    psum x1, waiting for transfers between devices, shards(): summed_q = lax.psum(partial_q, 'tok').astype(jnp.float32)  25.8 us
    all_to_all x1, blocking collectives, shards(): lax.all_to_all(tokens, 'tok', split_axis=1, concat_axis=0, tiled=True)  20.6 us
    all_to_all x1, blocking collectives, shards(): lax.all_to_all(partial_out.astype(jnp.bfloat16), 'tok', split_axis=0, con...  17.3 us
    convert_element_type x2, other arithmetic, shards(): updated = (fast_weights[0].astype(jnp.float32) - fast_rate[0][:, None, No...  11.9 us
    all_gather x1, blocking collectives, shards(): rates = lax.all_gather(step_sizes[0], 'tok', axis=0, tiled=True)  9.55 us
    dot_general x2, matrix products, newton_step(): jnp.einsum('mij,mjk->mik', cubic_term.astype(jnp.bfloat16), gram_matrix,...  9.35 us
    unnamed x30, local copies, waits for them, and re-layouts  8.54 us
  transfers between devices with their start and end apart: 4, of which 4 were waited for; matrix products, arithmetic and copies ran while one was open for 7% of the time, Pallas kernels for 0%

profile of v1, /device:TPU:0, one launch (start us, length us, event | category | flops | bytes accessed | tf_op | source)
XLA Modules:
  0.0 355.7 jit_solution(16210271070615239816)
XLA Ops:
  8.8 20.6 %all_to_all.38 = bf16[128,4,512]{2,0,1:T(8,128)(2,1)S(1)} all-to-all(bf16[128,4,512]{2,0,1:T(8,128)(2,1)S(1)} %copy.160), channel_id=1, replica_groups=mesh['section'=4,'tok'=4,'head'=2] {'tok'}, dimensions={1} | all-to-all | bytes 1048576 | tf_op jit(solution)/shard_map/all_to_all | solution.py:80
  32.8 3.0 convert_bitcast_fusion
  35.8 2.4 copy.161
  38.3 3.9 %copy.207 = bf16[1,2,3,512,512]{4,3,1,2,0:T(8,128)(2,1)} copy(bf16[1,2,3,512,512]{4,3,2,1,0:T(8,128)(2,1)} %param.12) | data formatting | bytes 6291456 | tf_op args[4]
  42.4 2.8 copy_convert_fusion
  45.2 3.4 copy.158
  48.6 9.5 %all-gather.1 = f32[1,512,2]{1,2,0:T(2,128)S(1)} all-gather(f32[1,128,2]{1,2,0:T(2,128)S(1)} %copy-done.12), channel_id=3, replica_groups=mesh['section'=4,'tok'=4,'head'=2] {'tok'}, dimensions={1}, use_global_device_ids=true | all-gather | bytes 5120 | tf_op jit(solution)/shard_map/all_gather | solution.py:82
  58.2 25.8 %all-reduce.2.cloned.1.call-done = bf16[512,2,512]{2,0,1:T(8,128)(2,1)} async-done(((bf16[512,2,512]{2,0,1:T(8,128)(2,1)}), bf16[512,2,512]{2,0,1:T(8,128)(2,1)}) %all-reduce.2.cloned.1.call-update) | async-done | bytes 1048592 | tf_op jit(solution)/shard_map/psum | solution.py:90
  85.5 149.0 %all-gather.4.cloned.1.call-done = bf16[8,512,1024]{2,1,0:T(8,128)(2,1)} async-done(((bf16[2,512,1024]{2,1,0:T(8,128)(2,1)}), bf16[8,512,1024]{2,1,0:T(8,128)(2,1)}) %all-gather.4.cloned.1.call-update) | async-done | bytes 8388624 | tf_op jit(solution)/shard_map/all_gather | solution.py:89
  234.4 6.3 %reduce_sum.48 = bf16[2,512,1024]{2,1,0:T(8,128)(2,1)S(1)} reduce(bf16[4,2,512,1024]{3,2,1,0:T(8,128)(2,1)} %bitcast.197, bf16[]{:T(256)} %constant.9.clone.1), dimensions={0}, to_apply=%region_0.0 | reduce | flops 3145728 | bytes 10485762 | tf_op jit(solution)/shard_map/reduce_sum | solution.py:89
  240.8 2.4 slice_convert_fusion
  253.5 2.9 copy.190
  256.4 2.8 fusion.44
  264.3 2.2 fusion.2
  266.5 3.4 copy.170
  270.0 6.4 %fusion.4 = bf16[6,512,512]{2,1,0:T(8,128)(2,1)S(1)} fusion(f32[2,3,512,512]{3,2,1,0:T(8,128)} %copy.170, f32[1,2,3,512,512]{4,3,2,1,0:T(8,128)} %copy.158, f32[6]{0:T(128)S(1)} %add.83, f32[6]{0:T(128)S(1)} %mul.145), kind=kLoop, calls=%fused_computation.7 | loop fusion | flops 6291456 | bytes 15728688 | tf_op jit(solution)/shard_map/convert_element_type | solution.py:101
  278.2 4.5 %fusion.63 = f32[6,512,512]{2,1,0:T(8,128)} fusion(bf16[6,512,512]{2,1,0:T(8,128)(2,1)S(1)} %fusion.4, bf16[6,512,512]{2,1,0:T(8,128)(2,1)S(1)} %convolution_convert_fusion.1), kind=kOutput, calls=%fused_computation.96 | convolution fusion | flops 1610612736 | bytes 12582912 | tf_op jit(solution)/shard_map/mij,mjk->mik/dot_general | solution.py:47
  282.7 6.9 %add_convert_fusion.1 = bf16[6,512,512]{2,1,0:T(8,128)(2,1)S(1)} fusion(f32[6,512,512]{2,1,0:T(8,128)} %fusion.63, bf16[6,512,512]{2,1,0:T(8,128)(2,1)S(1)} %fusion.4, bf16[6,512,512]{2,1,0:T(8,128)(2,1)S(1)} %convolution_convert_fusion.1), kind=kOutput, calls=%fused_computation.14 | convolution fusion | flops 1623195648 | bytes 15728640 | tf_op jit(solution)/shard_map/mij,mjk->mik/dot_general | solution.py:50
  293.2 2.5 fusion.7
  295.7 5.4 %fusion.6 = bf16[2,3,512,512]{3,2,0,1:T(8,128)(2,1)S(1)} fusion(f32[2,3,512,512]{3,2,1,0:T(8,128)S(1)} %bitcast.190, f32[2]{0:T(128)S(1)} %bitcast.210, bf16[1,2,3,512,512]{4,3,2,1,0:T(8,128)(2,1)} %param.12), kind=kLoop, calls=%fused_computation.11 | loop fusion | flops 6291456 | bytes 12582920 | tf_op jit(solution)/shard_map/convert_element_type | solution.py:109
  304.9 5.1 %fusion.20 = (f32[512,2]{0,1:T(2,128)S(1)}, f32[2,512,512]{2,1,0:T(8,128)}) fusion(f32[2,512,512]{1,2,0:T(8,128)} %fusion.41, bf16[2,3,512,512]{3,2,0,1:T(8,128)(2,1)} %copy-done.5, bf16[512,2,512]{2,0,1:T(8,128)(2,1)S(1)} %copy-done.6, f32[512,2]{0,1:T(2,128)S(1)} %add_rsqrt_fusion.1), kind=kOutput, calls=%fused_computation.32 | convolution fusion | flops 1079507968 | bytes 7348224 | tf_op jit(solution)/shard_map/thj,hij->thi/dot_general | solution.py:69
  312.7 17.3 %all_to_all.39 = bf16[4,128,512]{2,1,0:T(8,128)(2,1)S(1)} all-to-all(bf16[4,128,512]{2,1,0:T(8,128)(2,1)S(1)} %bitcast.207), channel_id=1, replica_groups=mesh['section'=4,'tok'=4,'head'=2] {'tok'}, dimensions={0} | all-to-all | bytes 1048576 | tf_op jit(solution)/shard_map/all_to_all | solution.py:112
  330.9 7.1 %reduce-scatter.2.cloned.1.call-done = bf16[128,1024]{1,0:T(8,128)(2,1)} async-done(((bf16[128,2048]{1,0:T(8,128)(2,1)}), bf16[128,1024]{1,0:T(8,128)(2,1)}) %reduce-scatter.2.cloned.1.call-update) | async-done | bytes 262160 | tf_op jit(solution)/shard_map/reduce_scatter | solution.py:115
  340.7 6.5 %subtract_convert_fusion = bf16[1,2,3,512,512]{4,3,2,1,0:T(8,128)(2,1)} fusion(f32[1,2,3,512,512]{4,3,2,1,0:T(8,128)} %bitcast.191, bf16[1,2,3,512,512]{4,3,2,1,0:T(8,128)(2,1)} %param.12, f32[2]{0:T(128)S(1)} %bitcast.211), kind=kLoop, calls=%fused_computation.12 | loop fusion | flops 6291456 | bytes 12582920 | tf_op jit(solution)/shard_map/convert_element_type | solution.py:109
  (67 shorter events, 39.7 us)
Async XLA Ops:
  7.2 304.7 %copy-start = (bf16[1,1024,512]{2,1,0:T(8,128)(2,1)S(1)}, bf16[1,1024,512]{2,1,0:T(8,128)(2,1)}, u32[]{:S(2)}) copy-start(bf16[1,1024,512]{2,1,0:T(8,128)(2,1)} %param.10) | copy-start | bytes 3145732
  7.2 76.8 %all-reduce.2.cloned.1.call-start = ((), (), s32[]{:S(2)}) async-start(), calls=%async_computation.3 | async-start | bytes 2097152 | tf_op jit(solution)/shard_map/psum | solution.py:90
  29.5 3.3 copy-start.10
  32.8 201.7 %all-gather.4.cloned.1.call-start = ((), (), s32[]{:S(2)}) async-start(), calls=%async_computation.5 | async-start | bytes 10485760 | tf_op jit(solution)/shard_map/all_gather | solution.py:89
  38.3 4.0 %copy-start.13 = (f32[1,2]{1,0:T(1,128)S(1)}, f32[1,2]{1,0:T(1,128)}, u32[]{:S(2)}) copy-start(f32[1,2]{1,0:T(1,128)} %param.14) | copy-start | bytes 28
  38.3 299.7 %reduce-scatter.2.cloned.1.call-start = ((), (), s32[]{:S(2)}) async-start(), calls=%async_computation.4 | async-start | bytes 786432 | tf_op jit(solution)/shard_map/reduce_scatter | solution.py:115
  45.2 3.4 copy-start.12
  246.9 2.5 copy-start.3
  256.4 2.8 copy-start.7
  259.2 1.6 copy-start.8
  260.8 1.6 copy-start.4
  262.4 1.9 copy-start.2
  293.2 2.5 copy-start.11
  295.7 5.4 %copy-start.1 = (f32[6,512,512]{2,1,0:T(8,128)}, f32[6,512,512]{2,1,0:T(8,128)S(1)}, u32[]{:S(2)}) copy-start(f32[6,512,512]{2,1,0:T(8,128)S(1)} %fusion.7) | copy-start | bytes 18874372
  295.7 7.1 %copy-start.6 = (bf16[512,2,512]{2,0,1:T(8,128)(2,1)S(1)}, bf16[512,2,512]{2,0,1:T(8,128)(2,1)}, u32[]{:S(2)}) copy-start(bf16[512,2,512]{2,0,1:T(8,128)(2,1)} %all-reduce.2.cloned.1.call-done) | copy-start | bytes 3145732
  301.1 1.7 copy-start.5
  311.9 26.1 %copy-start.9 = (bf16[1,128,2048]{2,1,0:T(8,128)(2,1)S(1)}, bf16[1,128,2048]{2,1,0:T(8,128)(2,1)}, u32[]{:S(2)}) copy-start(bf16[1,128,2048]{2,1,0:T(8,128)(2,1)} %param.8) | copy-start | bytes 1572868
  339.0 9.5 %collective-permute-start = (bf16[1,128,1024]{2,1,0:T(8,128)(2,1)S(1)}, bf16[1,128,1024]{2,1,0:T(8,128)(2,1)S(1)}, u32[]{:S(2)}, u32[]{:S(2)}) collective-permute-start(bf16[1,128,1024]{2,1,0:T(8,128)(2,1)S(1)} %fusion.56), channel_id=1, source_target_pairs={{0,8},{8,16},{16,24},{24,0},{1,9},{9,17},{17,25},{25,1},{2,10},{10... | collective-permute-start | bytes 786440 | tf_op jit(solution)/shard_map/ppermute | solution.py:15
Sparse Core Ops, SparseCore 0:
  32.9 51.0 all-reduce.1
  85.5 148.8 all-gather.3
  331.0 6.9 reduce-scatter.1
